TPU v7x, 512 devices: a whole 4x8x8 slice. The times are simulated.
512 devices in a mesh: leaf: 128 (over y, z, core), rhs: 4 (over x).
Axes of the slice: x: 4, y: 8, z: 8, core: 2. Of those that a mesh axis runs over, the one named last changes fastest.
Arguments:
- rhs_block: float32 [65536, 1024], P('leaf', 'rhs'), may hold values from -6 to 6
- leaf_order: int32 [128, 512], P('leaf'), may hold values from 0 to 511, as said below
- leaf_inverse: float32 [65536, 512], P('leaf'), may hold values from -0.04 to 3, as said below
- leaf_basis: float32 [65536, 128], P('leaf'), may hold values from -0.09678524 to 0.09678524
- transfer: bfloat16 [128, 6, 128, 128], P('leaf'), may hold values from -0.05 to 1.25, as said below
- precision: bfloat16 [128, 7, 128, 128], P('leaf'), may hold values from -0.09 to 8, as said below
Outputs:
- solution: float32 [65536, 1024], P('leaf', 'rhs')
Inputs may be any that keep to these rules, and one draw needn't show every extreme that they name: `leaf_order`: each row is a permutation of 0 to 511. `leaf_inverse`: each leaf's block of 512 x 512 entries is symmetric positive definite. transfer[b, k] is the same for all leaves b of one aligned group of 2 ** (k + 1) leaves. Every block is symmetric positive definite; precision[b, k] is the same for all leaves b of one aligned group of 2 ** (k + 1) leaves.
All inputs are finite; a program needn't handle non-finite values.
Results may differ from a plain program's by a relative error of at most 0.0003.
Values sent between devices are 32-bit elements; how exact they have to be, the bound alone decides.
A program may use at most 64 MiB of HBM per device.

v0:
```python
import jax
import jax.numpy as jnp
from jax import lax
from jax.sharding import PartitionSpec as P


def from_partner(block, axis, apart):
    count = lax.axis_size(axis)
    route = []
    for low in range(count):
        high = low | 1 << apart
        if high != low and high < count:
            route += [(low, high), (high, low)]
    return lax.ppermute(block, axis, route)


def product(left_op, right_op):
    return jnp.dot(
        left_op, right_op, precision=lax.Precision.HIGHEST, preferred_element_type=jnp.float32
    )


def cholesky_solve(matrix, right_side):
    factor = jnp.linalg.cholesky(matrix)
    middle = lax.linalg.triangular_solve(factor, right_side, left_side=True, lower=True)
    return lax.linalg.triangular_solve(factor, middle, left_side=True, lower=True, transpose_a=True)


def body(rhs_block, leaf_order, leaf_inverse, leaf_basis, transfer, precision):
    point_order = leaf_order[0]
    ordered = jnp.take(rhs_block, point_order, axis=0)
    columns = rhs_block.shape[1]
    rank_size = leaf_basis.shape[1]
    solved = product(leaf_inverse, ordered)
    projected = product(leaf_basis.T, solved)
    levels = lax.axis_size("leaf").bit_length() - 1
    col_width = rank_size // lax.axis_size("rhs")
    col_start = lax.axis_index("rhs") * col_width
    carried = product(leaf_inverse, leaf_basis)
    gram_full = product(leaf_basis.T, carried)
    gram_part = lax.dynamic_slice_in_dim(gram_full, col_start, col_width, 1)
    for height in range(levels):
        other_proj, other_part = from_partner((projected, gram_part), "leaf", height)
        whole_gram = lax.all_gather(gram_part + other_part, "rhs", axis=1, tiled=True)
        summed = projected + other_proj
        coupling = precision[0, height].astype(jnp.float32)
        coeffs = cholesky_solve(coupling + whole_gram, jnp.concatenate([summed, coupling], axis=1))
        coef_rhs = coeffs[:, :columns]
        coef_basis = coeffs[:, columns:]
        solved = solved - product(carried, coef_rhs)
        if height + 1 < levels:
            mixer = transfer[0, height].astype(jnp.float32)
            update = product(coef_basis, mixer)
            carried = product(carried, update)
            projected = product(mixer.T, product(coupling, coef_rhs))
            left_part = product(mixer.T, product(coef_basis.T, whole_gram))
            gram_part = product(left_part, lax.dynamic_slice_in_dim(mixer, col_start, col_width, 1))
    return jnp.zeros_like(solved).at[point_order].set(solved)


def solution(mesh):
    placed = (
        P("leaf", "rhs"),
        P("leaf", None),
        P("leaf", None),
        P("leaf", None),
        P("leaf", None, None, None),
        P("leaf", None, None, None),
    )
    return jax.shard_map(
        body, mesh=mesh, in_specs=placed, out_specs=P("leaf", "rhs"), check_vma=False
    )
```

profile of v0, /device:TPU:4, one launch (start us, length us, event | category | flops | bytes accessed | tf_op | source)
XLA Modules:
  0.0 343.0 jit_solution(16715792062917091727)
XLA Ops:
  0.0 0.8 compare_select_fusion
  0.8 0.7 copy-done.14
  1.5 2.6 gather_fusion
  4.1 2.0 fusion
  6.7 1.9 collective-permute-start.1
  8.6 1.0 fusion.204
  10.2 2.4 collective-permute-start
  13.0 0.7 copy-done.1
  13.6 0.7 fusion.203
  14.4 0.6 bitcast_convert_fusion.4
  15.2 0.6 bitcast_convert_fusion.3
  15.9 0.6 bitcast_convert_fusion.2
  16.8 0.6 bitcast_convert_fusion
  17.5 15.9 %all_gather.21 = f32[128,128]{0,1:T(8,128)S(1)} all-gather(f32[128,32]{0,1:T(8,128)S(1)} %fusion.270), channel_id=1, replica_groups=mesh['leaf'=128,'rhs'=4] {'rhs'}, dimensions={1}, use_global_device_ids=true | all-gather | bytes 81920 | tf_op jit(solution)/shard_map/all_gather | solution.py:44
  33.5 11.7 %cholesky.119 = f32[128,128]{1,0:T(8,128)S(1)} custom-call(f32[128,128]{1,0:T(8,128)S(1)} %fusion.84), custom_call_target="Cholesky" | custom-call | tf_op jit(solution)/shard_map/jit(cholesky)/cholesky | solution.py:24
  45.2 0.7 compare_reduce_fusion.6
  46.6 9.8 %custom-call.21 = f32[1,128,128]{1,2,0:T(8,128)S(1)} custom-call(f32[1,128,128]{2,1,0:T(8,128)S(1)} %fusion.50), custom_call_target="InvertDiagBlocksLowerTriangular" | custom-call | tf_op jit(solution)/shard_map/triangular_solve/custom-call.2 | solution.py:26
  59.9 1.9 collective-permute-start.2
  62.1 3.9 %collective-permute-start.3 = (f32[128,256]{0,1:T(8,128)S(1)}, f32[128,256]{0,1:T(8,128)S(1)}, u32[]{:S(2)}, u32[]{:S(2)}) collective-permute-start(f32[128,256]{0,1:T(8,128)S(1)} %convolution_bitcast_fusion.6), channel_id=1, source_target_pairs={{0,8},{8,0},{4,12},{12,4},{16,24},{24,16},{20,28},{28,20},{32,40},... | collective-permute-start | bytes 393224 | tf_op jit(solution)/shard_map/ppermute | solution.py:14
  66.0 12.1 %all_gather.22 = f32[128,128]{0,1:T(8,128)S(1)} all-gather(f32[128,32]{0,1:T(8,128)S(1)} %add.112), channel_id=1, replica_groups=mesh['leaf'=128,'rhs'=4] {'rhs'}, dimensions={1}, use_global_device_ids=true | all-gather | bytes 81920 | tf_op jit(solution)/shard_map/all_gather | solution.py:44
  78.3 11.7 %cholesky.130 = f32[128,128]{1,0:T(8,128)S(1)} custom-call(f32[128,128]{1,0:T(8,128)S(1)} %fusion.80), custom_call_target="Cholesky" | custom-call | tf_op jit(solution)/shard_map/jit(cholesky)/cholesky | solution.py:24
  90.0 0.7 compare_reduce_fusion.5
  90.7 0.6 fusion.51
  91.3 9.8 %custom-call.23 = f32[1,128,128]{1,2,0:T(8,128)S(1)} custom-call(f32[1,128,128]{2,1,0:T(8,128)S(1)} %fusion.51), custom_call_target="InvertDiagBlocksLowerTriangular" | custom-call | tf_op jit(solution)/shard_map/triangular_solve/custom-call.2 | solution.py:26
  104.7 1.9 collective-permute-start.4
  106.8 4.8 %collective-permute-start.5 = (f32[128,256]{0,1:T(8,128)S(1)}, f32[128,256]{0,1:T(8,128)S(1)}, u32[]{:S(2)}, u32[]{:S(2)}) collective-permute-start(f32[128,256]{0,1:T(8,128)S(1)} %convolution_bitcast_fusion.5), channel_id=1, source_target_pairs={{0,16},{16,0},{4,20},{20,4},{8,24},{24,8},{12,28},{28,12},{32,48},... | collective-permute-start | bytes 393224 | tf_op jit(solution)/shard_map/ppermute | solution.py:14
  111.7 12.3 %all_gather.23 = f32[128,128]{0,1:T(8,128)S(1)} all-gather(f32[128,32]{0,1:T(8,128)S(1)} %add.115), channel_id=1, replica_groups=mesh['leaf'=128,'rhs'=4] {'rhs'}, dimensions={1}, use_global_device_ids=true | all-gather | bytes 81920 | tf_op jit(solution)/shard_map/all_gather | solution.py:44
  124.1 11.7 %cholesky.141 = f32[128,128]{1,0:T(8,128)S(1)} custom-call(f32[128,128]{1,0:T(8,128)S(1)} %fusion.76), custom_call_target="Cholesky" | custom-call | tf_op jit(solution)/shard_map/jit(cholesky)/cholesky | solution.py:24
  135.9 0.7 compare_reduce_fusion.4
  136.6 0.7 fusion.52
  137.3 9.8 %custom-call.25 = f32[1,128,128]{1,2,0:T(8,128)S(1)} custom-call(f32[1,128,128]{2,1,0:T(8,128)S(1)} %fusion.52), custom_call_target="InvertDiagBlocksLowerTriangular" | custom-call | tf_op jit(solution)/shard_map/triangular_solve/custom-call.2 | solution.py:26
  147.2 0.8 copy-done.6
  151.5 5.9 %collective-permute-start.6 = (f32[128,32]{0,1:T(8,128)S(1)}, f32[128,32]{0,1:T(8,128)S(1)}, u32[]{:S(2)}, u32[]{:S(2)}) collective-permute-start(f32[128,32]{0,1:T(8,128)S(1)} %fusion.133), channel_id=1, source_target_pairs={{0,32},{32,0},{4,36},{36,4},{8,40},{40,8},{12,44},{44,12},{16,48},... | collective-permute-start | bytes 49160 | tf_op jit(solution)/shard_map/ppermute | solution.py:14
  157.6 3.9 %collective-permute-start.7 = (f32[128,256]{0,1:T(8,128)S(1)}, f32[128,256]{0,1:T(8,128)S(1)}, u32[]{:S(2)}, u32[]{:S(2)}) collective-permute-start(f32[128,256]{0,1:T(8,128)S(1)} %convolution_bitcast_fusion.4), channel_id=1, source_target_pairs={{0,32},{32,0},{4,36},{36,4},{8,40},{40,8},{12,44},{44,12},{16,48},... | collective-permute-start | bytes 393224 | tf_op jit(solution)/shard_map/ppermute | solution.py:14
  161.5 12.0 %all_gather.24 = f32[128,128]{0,1:T(8,128)S(1)} all-gather(f32[128,32]{0,1:T(8,128)S(1)} %add.118), channel_id=1, replica_groups=mesh['leaf'=128,'rhs'=4] {'rhs'}, dimensions={1}, use_global_device_ids=true | all-gather | bytes 81920 | tf_op jit(solution)/shard_map/all_gather | solution.py:44
  173.7 11.7 %cholesky.152 = f32[128,128]{1,0:T(8,128)S(1)} custom-call(f32[128,128]{1,0:T(8,128)S(1)} %fusion.72), custom_call_target="Cholesky" | custom-call | tf_op jit(solution)/shard_map/jit(cholesky)/cholesky | solution.py:24
  185.4 0.6 compare_reduce_fusion.3
  186.0 0.7 fusion.53
  186.7 9.8 %custom-call.27 = f32[1,128,128]{1,2,0:T(8,128)S(1)} custom-call(f32[1,128,128]{2,1,0:T(8,128)S(1)} %fusion.53), custom_call_target="InvertDiagBlocksLowerTriangular" | custom-call | tf_op jit(solution)/shard_map/triangular_solve/custom-call.2 | solution.py:26
  196.6 0.8 copy-done.5
  200.8 1.9 collective-permute-start.8
  203.0 3.9 %collective-permute-start.9 = (f32[128,256]{0,1:T(8,128)S(1)}, f32[128,256]{0,1:T(8,128)S(1)}, u32[]{:S(2)}, u32[]{:S(2)}) collective-permute-start(f32[128,256]{0,1:T(8,128)S(1)} %convolution_bitcast_fusion.3), channel_id=1, source_target_pairs={{0,64},{64,0},{4,68},{68,4},{8,72},{72,8},{12,76},{76,12},{16,80},... | collective-permute-start | bytes 393224 | tf_op jit(solution)/shard_map/ppermute | solution.py:14
  207.0 12.1 %all_gather.25 = f32[128,128]{0,1:T(8,128)S(1)} all-gather(f32[128,32]{0,1:T(8,128)S(1)} %add.121), channel_id=1, replica_groups=mesh['leaf'=128,'rhs'=4] {'rhs'}, dimensions={1}, use_global_device_ids=true | all-gather | bytes 81920 | tf_op jit(solution)/shard_map/all_gather | solution.py:44
  219.2 11.7 %cholesky.163 = f32[128,128]{1,0:T(8,128)S(1)} custom-call(f32[128,128]{1,0:T(8,128)S(1)} %fusion.68), custom_call_target="Cholesky" | custom-call | tf_op jit(solution)/shard_map/jit(cholesky)/cholesky | solution.py:24
  230.9 0.6 compare_reduce_fusion.2
  231.6 0.7 fusion.54
  232.2 9.8 %custom-call.29 = f32[1,128,128]{1,2,0:T(8,128)S(1)} custom-call(f32[1,128,128]{2,1,0:T(8,128)S(1)} %fusion.54), custom_call_target="InvertDiagBlocksLowerTriangular" | custom-call | tf_op jit(solution)/shard_map/triangular_solve/custom-call.2 | solution.py:26
  242.1 0.8 copy-done.4
  246.4 2.5 collective-permute-start.10
  249.1 4.2 %collective-permute-start.11 = (f32[128,256]{0,1:T(8,128)S(1)}, f32[128,256]{0,1:T(8,128)S(1)}, u32[]{:S(2)}, u32[]{:S(2)}) collective-permute-start(f32[128,256]{0,1:T(8,128)S(1)} %convolution_bitcast_fusion.2), channel_id=1, source_target_pairs={{0,128},{128,0},{4,132},{132,4},{8,136},{136,8},{12,140},{140,12},... | collective-permute-start | bytes 393224 | tf_op jit(solution)/shard_map/ppermute | solution.py:14
  253.4 12.1 %all_gather.26 = f32[128,128]{0,1:T(8,128)S(1)} all-gather(f32[128,32]{0,1:T(8,128)S(1)} %add.124), channel_id=1, replica_groups=mesh['leaf'=128,'rhs'=4] {'rhs'}, dimensions={1}, use_global_device_ids=true | all-gather | bytes 81920 | tf_op jit(solution)/shard_map/all_gather | solution.py:44
  265.6 11.7 %cholesky.174 = f32[128,128]{1,0:T(8,128)S(1)} custom-call(f32[128,128]{1,0:T(8,128)S(1)} %fusion.64), custom_call_target="Cholesky" | custom-call | tf_op jit(solution)/shard_map/jit(cholesky)/cholesky | solution.py:24
  277.4 0.6 compare_reduce_fusion.1
  278.0 0.7 fusion.55
  278.7 9.8 %custom-call.31 = f32[1,128,128]{1,2,0:T(8,128)S(1)} custom-call(f32[1,128,128]{2,1,0:T(8,128)S(1)} %fusion.55), custom_call_target="InvertDiagBlocksLowerTriangular" | custom-call | tf_op jit(solution)/shard_map/triangular_solve/custom-call.2 | solution.py:26
  292.0 5.8 %collective-permute-start.12 = (f32[128,32]{0,1:T(8,128)S(1)}, f32[128,32]{0,1:T(8,128)S(1)}, u32[]{:S(2)}, u32[]{:S(2)}) collective-permute-start(f32[128,32]{0,1:T(8,128)S(1)} %fusion.115), channel_id=1, source_target_pairs={{0,256},{256,0},{4,260},{260,4},{8,264},{264,8},{12,268},{268,12},... | collective-permute-start | bytes 49160 | tf_op jit(solution)/shard_map/ppermute | solution.py:14
  298.0 4.0 %collective-permute-start.13 = (f32[128,256]{0,1:T(8,128)S(1)}, f32[128,256]{0,1:T(8,128)S(1)}, u32[]{:S(2)}, u32[]{:S(2)}) collective-permute-start(f32[128,256]{0,1:T(8,128)S(1)} %convolution_bitcast_fusion.1), channel_id=1, source_target_pairs={{0,256},{256,0},{4,260},{260,4},{8,264},{264,8},{12,268},{268,12},... | collective-permute-start | bytes 393224 | tf_op jit(solution)/shard_map/ppermute | solution.py:14
  302.0 12.2 %all_gather.27 = f32[128,128]{0,1:T(8,128)S(1)} all-gather(f32[128,32]{0,1:T(8,128)S(1)} %add.127), channel_id=1, replica_groups=mesh['leaf'=128,'rhs'=4] {'rhs'}, dimensions={1}, use_global_device_ids=true | all-gather | bytes 81920 | tf_op jit(solution)/shard_map/all_gather | solution.py:44
  314.3 11.7 %cholesky.185 = f32[128,128]{1,0:T(8,128)S(1)} custom-call(f32[128,128]{1,0:T(8,128)S(1)} %fusion.60), custom_call_target="Cholesky" | custom-call | tf_op jit(solution)/shard_map/jit(cholesky)/cholesky | solution.py:24
  326.1 0.6 compare_reduce_fusion
  326.7 0.7 fusion.56
  327.4 9.8 %custom-call.33 = f32[1,128,128]{1,2,0:T(8,128)S(1)} custom-call(f32[1,128,128]{2,1,0:T(8,128)S(1)} %fusion.56), custom_call_target="InvertDiagBlocksLowerTriangular" | custom-call | tf_op jit(solution)/shard_map/triangular_solve/custom-call.2 | solution.py:26
  337.2 0.8 copy-done.7
  339.4 3.0 scatter_custom_fusion
  (161 shorter events, 27.0 us)
Async XLA Ops:
  0.0 4.1 %copy-start = (f32[512,512]{1,0:T(8,128)S(1)}, f32[512,512]{1,0:T(8,128)}, u32[]{:S(2)}) copy-start(f32[512,512]{1,0:T(8,128)} %param.13) | copy-start | bytes 3145732
  0.8 0.7 copy-start.14
  4.1 2.0 copy-start.2
  6.7 49.7 %collective-permute-start.1 = (f32[128,256]{0,1:T(8,128)S(1)}, f32[128,256]{0,1:T(8,128)S(1)}, u32[]{:S(2)}, u32[]{:S(2)}) collective-permute-start(f32[128,256]{0,1:T(8,128)S(1)} %convolution_bitcast_fusion), channel_id=1, source_target_pairs={{0,4},{4,0},{8,12},{12,8},{16,20},{20,16},{24,28},{28,24},{32,36},... | collective-permute-start | bytes 393224 | tf_op jit(solution)/shard_map/ppermute | solution.py:14
  9.6 3.0 copy-start.3
  10.2 7.2 %collective-permute-start = (f32[128,32]{0,1:T(8,128)S(1)}, f32[128,32]{0,1:T(8,128)S(1)}, u32[]{:S(2)}, u32[]{:S(2)}) collective-permute-start(f32[128,32]{0,1:T(8,128)S(1)} %dynamic-slice_bitcast_fusion), channel_id=1, source_target_pairs={{0,4},{4,0},{8,12},{12,8},{16,20},{20,16},{24,28},{28,24},{32,36},... | collective-permute-start | bytes 49160 | tf_op jit(solution)/shard_map/ppermute | solution.py:14
  12.7 0.9 copy-start.1
  58.9 0.8 copy-start.13
  59.9 6.1 %collective-permute-start.2 = (f32[128,32]{0,1:T(8,128)S(1)}, f32[128,32]{0,1:T(8,128)S(1)}, u32[]{:S(2)}, u32[]{:S(2)}) collective-permute-start(f32[128,32]{0,1:T(8,128)S(1)} %fusion.145), channel_id=1, source_target_pairs={{0,8},{8,0},{4,12},{12,4},{16,24},{24,16},{20,28},{28,20},{32,40},... | collective-permute-start | bytes 49160 | tf_op jit(solution)/shard_map/ppermute | solution.py:14
  62.1 39.1 %collective-permute-start.3 = (f32[128,256]{0,1:T(8,128)S(1)}, f32[128,256]{0,1:T(8,128)S(1)}, u32[]{:S(2)}, u32[]{:S(2)}) collective-permute-start(f32[128,256]{0,1:T(8,128)S(1)} %convolution_bitcast_fusion.6), channel_id=1, source_target_pairs={{0,8},{8,0},{4,12},{12,4},{16,24},{24,16},{20,28},{28,20},{32,40},... | collective-permute-start | bytes 393224 | tf_op jit(solution)/shard_map/ppermute | solution.py:14
  103.7 0.8 copy-start.12
  104.7 7.0 %collective-permute-start.4 = (f32[128,32]{0,1:T(8,128)S(1)}, f32[128,32]{0,1:T(8,128)S(1)}, u32[]{:S(2)}, u32[]{:S(2)}) collective-permute-start(f32[128,32]{0,1:T(8,128)S(1)} %fusion.139), channel_id=1, source_target_pairs={{0,16},{16,0},{4,20},{20,4},{8,24},{24,8},{12,28},{28,12},{32,48},... | collective-permute-start | bytes 49160 | tf_op jit(solution)/shard_map/ppermute | solution.py:14
  106.8 40.3 %collective-permute-start.5 = (f32[128,256]{0,1:T(8,128)S(1)}, f32[128,256]{0,1:T(8,128)S(1)}, u32[]{:S(2)}, u32[]{:S(2)}) collective-permute-start(f32[128,256]{0,1:T(8,128)S(1)} %convolution_bitcast_fusion.5), channel_id=1, source_target_pairs={{0,16},{16,0},{4,20},{20,4},{8,24},{24,8},{12,28},{28,12},{32,48},... | collective-permute-start | bytes 393224 | tf_op jit(solution)/shard_map/ppermute | solution.py:14
  147.1 0.8 copy-start.6
  150.5 0.8 copy-start.11
  151.5 10.0 %collective-permute-start.6 = (f32[128,32]{0,1:T(8,128)S(1)}, f32[128,32]{0,1:T(8,128)S(1)}, u32[]{:S(2)}, u32[]{:S(2)}) collective-permute-start(f32[128,32]{0,1:T(8,128)S(1)} %fusion.133), channel_id=1, source_target_pairs={{0,32},{32,0},{4,36},{36,4},{8,40},{40,8},{12,44},{44,12},{16,48},... | collective-permute-start | bytes 49160 | tf_op jit(solution)/shard_map/ppermute | solution.py:14
  157.6 39.0 %collective-permute-start.7 = (f32[128,256]{0,1:T(8,128)S(1)}, f32[128,256]{0,1:T(8,128)S(1)}, u32[]{:S(2)}, u32[]{:S(2)}) collective-permute-start(f32[128,256]{0,1:T(8,128)S(1)} %convolution_bitcast_fusion.4), channel_id=1, source_target_pairs={{0,32},{32,0},{4,36},{36,4},{8,40},{40,8},{12,44},{44,12},{16,48},... | collective-permute-start | bytes 393224 | tf_op jit(solution)/shard_map/ppermute | solution.py:14
  196.5 0.8 copy-start.5
  199.8 0.8 copy-start.10
  200.8 6.1 %collective-permute-start.8 = (f32[128,32]{0,1:T(8,128)S(1)}, f32[128,32]{0,1:T(8,128)S(1)}, u32[]{:S(2)}, u32[]{:S(2)}) collective-permute-start(f32[128,32]{0,1:T(8,128)S(1)} %fusion.127), channel_id=1, source_target_pairs={{0,64},{64,0},{4,68},{68,4},{8,72},{72,8},{12,76},{76,12},{16,80},... | collective-permute-start | bytes 49160 | tf_op jit(solution)/shard_map/ppermute | solution.py:14
  203.0 39.0 %collective-permute-start.9 = (f32[128,256]{0,1:T(8,128)S(1)}, f32[128,256]{0,1:T(8,128)S(1)}, u32[]{:S(2)}, u32[]{:S(2)}) collective-permute-start(f32[128,256]{0,1:T(8,128)S(1)} %convolution_bitcast_fusion.3), channel_id=1, source_target_pairs={{0,64},{64,0},{4,68},{68,4},{8,72},{72,8},{12,76},{76,12},{16,80},... | collective-permute-start | bytes 393224 | tf_op jit(solution)/shard_map/ppermute | solution.py:14
  242.0 0.8 copy-start.4
  245.4 0.8 copy-start.9
  246.4 7.0 %collective-permute-start.10 = (f32[128,32]{0,1:T(8,128)S(1)}, f32[128,32]{0,1:T(8,128)S(1)}, u32[]{:S(2)}, u32[]{:S(2)}) collective-permute-start(f32[128,32]{0,1:T(8,128)S(1)} %fusion.121), channel_id=1, source_target_pairs={{0,128},{128,0},{4,132},{132,4},{8,136},{136,8},{12,140},{140,12},... | collective-permute-start | bytes 49160 | tf_op jit(solution)/shard_map/ppermute | solution.py:14
  249.1 39.4 %collective-permute-start.11 = (f32[128,256]{0,1:T(8,128)S(1)}, f32[128,256]{0,1:T(8,128)S(1)}, u32[]{:S(2)}, u32[]{:S(2)}) collective-permute-start(f32[128,256]{0,1:T(8,128)S(1)} %convolution_bitcast_fusion.2), channel_id=1, source_target_pairs={{0,128},{128,0},{4,132},{132,4},{8,136},{136,8},{12,140},{140,12},... | collective-permute-start | bytes 393224 | tf_op jit(solution)/shard_map/ppermute | solution.py:14
  291.0 0.8 copy-start.8
  292.0 10.0 %collective-permute-start.12 = (f32[128,32]{0,1:T(8,128)S(1)}, f32[128,32]{0,1:T(8,128)S(1)}, u32[]{:S(2)}, u32[]{:S(2)}) collective-permute-start(f32[128,32]{0,1:T(8,128)S(1)} %fusion.115), channel_id=1, source_target_pairs={{0,256},{256,0},{4,260},{260,4},{8,264},{264,8},{12,268},{268,12},... | collective-permute-start | bytes 49160 | tf_op jit(solution)/shard_map/ppermute | solution.py:14
  298.0 39.2 %collective-permute-start.13 = (f32[128,256]{0,1:T(8,128)S(1)}, f32[128,256]{0,1:T(8,128)S(1)}, u32[]{:S(2)}, u32[]{:S(2)}) collective-permute-start(f32[128,256]{0,1:T(8,128)S(1)} %convolution_bitcast_fusion.1), channel_id=1, source_target_pairs={{0,256},{256,0},{4,260},{260,4},{8,264},{264,8},{12,268},{268,12},... | collective-permute-start | bytes 393224 | tf_op jit(solution)/shard_map/ppermute | solution.py:14
  337.2 0.8 copy-start.7
where the time goes:
time: 348 us; the launch traced here: 343 us
  other arithmetic  164 us (47%)
  blocking collectives  88.8 us (26%)
  starting transfers between devices  49.1 us (14%)
  matrix products  24 us (7%)
  local copies, waits for them, and re-layouts  15.5 us (4%)
    all_gather x7, blocking collectives, body(): lax.all_gather(gram_part + other_part, 'rhs', axis=1, tiled=True)  88.8 us
    another operation x21, other arithmetic, cholesky_solve(): factor = jnp.linalg.cholesky(matrix)  86.9 us
    another operation x14, other arithmetic, cholesky_solve(): lax.linalg.triangular_solve(factor, middle, left_side=True, lower=True, t...  73.3 us
    ppermute x14, starting transfers between devices, from_partner(): return lax.ppermute(block, axis, route)  49.1 us
    dot_general x53, matrix products, product(): jnp.dot(left_op, right_op, precision=lax.Precision.HIGHEST, preferred_ele...  19.2 us
    unnamed x37, local copies, waits for them, and re-layouts  8.33 us
  transfers between devices with their start and end apart: 14, of which 0 were waited for; matrix products, arithmetic and copies ran while one was open for 49% of the time, Pallas kernels for 0%

commit v1 on v0

v1 whole, which is shorter than its diff:
```python
import functools

import jax
import jax.numpy as jnp
from jax import lax
from jax.experimental import pallas as pl
from jax.experimental.pallas import tpu as pltpu
from jax.sharding import PartitionSpec as P

MESH = pl.DeviceIdType.MESH
F32 = jnp.float32
BF16 = jnp.bfloat16


def split(value):
    high = value.astype(BF16)
    return high, (value - high.astype(F32)).astype(BF16)


def dot(left, right, dims=((1,), (0,))):
    return lax.dot_general(left, right, (dims, ((), ())), preferred_element_type=F32)


def product(left, right, dims=((1,), (0,))):
    left_cat = jnp.concatenate([left[0], left[0], left[1]], axis=dims[0][0])
    right_cat = jnp.concatenate([right[0], right[1], right[0]], axis=dims[1][0])
    return dot(left_cat, right_cat, dims)


def inverse(blocks, ones):
    blocks = list(blocks)
    count = len(blocks)
    width = blocks[0].shape[1]
    sub = lax.broadcasted_iota(jnp.int32, (8, width), 0)
    lane = lax.broadcasted_iota(jnp.int32, (8, width), 1)
    for step in range(count):
        low = 8 * step
        rows = blocks[step]
        cols = [
            [jnp.broadcast_to(blocks[b][:, low + j : low + j + 1], (8, width)) for b in range(count)]
            for j in range(8)
        ]
        inside = (lane >= low) & (lane < low + 8)
        z = jnp.where(inside, jnp.where(lane - low == sub, 1.0, 0.0), rows)
        cb = [cols[k][step] * ones for k in range(8)]
        scale = ones
        for i in range(8):
            pivot = sub == i
            inv = 1.0 / jnp.broadcast_to(cb[i][i : i + 1, :], (8, width))
            m = jnp.where(pivot, 0.0, cb[i] * inv)
            scale = jnp.where(pivot, inv, scale)
            z = z - m * jnp.broadcast_to(z[i : i + 1, :], (8, width))
            for k in range(i + 1, 8):
                cb[k] = cb[k] - m * jnp.broadcast_to(cb[k][i : i + 1, :], (8, width))
        z = z * scale
        zr = [jnp.broadcast_to(z[j : j + 1, :], (8, width)) for j in range(8)]
        for turn in range(1, count):
            b = (step + turn) % count
            total = jnp.where(inside, 0.0, blocks[b])
            for j in range(8):
                total = total - cols[j][b] * zr[j]
            blocks[b] = total
        blocks[step] = z
    return blocks


def kernel(
    levels, rhs_ref, order_ref, inv_ref, basis_ref, transfer_ref, precision_ref, out_ref,
    gs, gr, ph, ps, pr, uh, ul, vh, vl, cc, minv, acc, mix, accr, zh, qin, onehot,
    ssem_g, rsem_g, ssem_p, rsem_p, sem_a,
):
    me = lax.axis_index("leaf")
    group = lax.axis_index("rhs")
    core = me % 2
    sibling = me + 1 - 2 * core

    def partner_of(apart, target):
        chip_partner = me + apart * (1 - 2 * ((me // apart) % 2))
        return (chip_partner // 2) * 2 + target

    def gram_copy(level, slot, target):
        return pltpu.make_async_remote_copy(
            src_ref=gs.at[level], dst_ref=gr.at[level], send_sem=ssem_g.at[level, slot], recv_sem=rsem_g.at[level],
            device_id=(target, group), device_id_type=MESH,
        )

    def proj_copy(level, target):
        return pltpu.make_async_remote_copy(
            src_ref=ps.at[level], dst_ref=pr.at[level], send_sem=ssem_p.at[level], recv_sem=rsem_p.at[level],
            device_id=(target, group), device_id_type=MESH,
        )

    barrier = pltpu.get_barrier_semaphore()
    pl.semaphore_signal(barrier, inc=1, device_id=(sibling, group), device_id_type=MESH)
    for level in range(1, levels):
        apart = 1 << level
        pl.semaphore_signal(barrier, inc=1, device_id=(partner_of(apart, 1), group), device_id_type=MESH)

        @pl.when(core == 0)
        def _():
            pl.semaphore_signal(barrier, inc=1, device_id=(partner_of(apart, 0), group), device_id_type=MESH)

    basis = split(basis_ref[...])
    leaf_inv = split(inv_ref[...])
    q = product(leaf_inv, basis)
    q_pair = split(q)
    gs[0] = product(basis, q_pair, ((0,), (0,)))

    @pl.when(core == 0)
    def _():
        pl.semaphore_wait(barrier, levels)

    @pl.when(core == 1)
    def _():
        pl.semaphore_wait(barrier, 2 * levels - 1)

    gram_copy(0, 0, sibling).start()

    points = rhs_ref.shape[0]
    order_row = order_ref[...]
    spread = lax.broadcasted_iota(jnp.int32, (points, points), 0) == order_row
    onehot[...] = jnp.where(spread, 1.0, 0.0).astype(BF16)
    q_in = (dot(onehot[...], q_pair[0]), dot(onehot[...], q_pair[1]))
    q_in = (q_in[0].astype(BF16), q_in[1].astype(BF16))
    qin[0] = q_in[0]
    qin[1] = q_in[1]
    rhs = split(rhs_ref[...])
    proj = product(q_in, rhs, ((0,), (0,)))
    ph[0] = proj[:, :128]
    ph[1] = proj[:, 128:]
    ps[0] = ph[1 - core]
    proj_copy(0, sibling).start()

    def tables(k, carry):
        mixer = transfer_ref[0, k]
        lam = precision_ref[0, k]
        u = dot(lam, mixer)
        v = dot(mixer, lam, ((0,), (0,)))
        u_pair = split(u)
        v_pair = split(v)
        uh[k] = u_pair[0]
        ul[k] = u_pair[1]
        vh[k] = v_pair[0]
        vl[k] = v_pair[1]
        cc[k] = dot(v_pair[0], mixer) + dot(v_pair[1], mixer)
        return carry

    lax.fori_loop(0, levels - 1, tables, 0)

    ordered = (
        dot(onehot[...], rhs[0], ((0,), (0,))).astype(BF16),
        dot(onehot[...], rhs[1], ((0,), (0,))).astype(BF16),
    )
    z = split(product(leaf_inv, ordered))
    z_in = dot(onehot[...], z[0]) + dot(onehot[...], z[1])
    zh[0] = z_in[:, :128]
    zh[1] = z_in[:, 128:]

    ones = jnp.where(zh[0, :8, :] == zh[0, :8, :], 1.0, 0.0)
    rank = acc.shape[0]
    acc[...] = jnp.zeros_like(acc)
    eye = lax.broadcasted_iota(jnp.int32, (rank, rank), 0) == lax.broadcasted_iota(jnp.int32, (rank, rank), 1)
    mix[...] = jnp.where(eye, 1.0, 0.0)

    def level_step(k, apart):
        gram_copy(k, 0, sibling).wait_recv()
        count = rank // 8
        blocks = []
        for b in range(count):
            at = pl.ds(8 * b, 8)
            blocks.append(precision_ref[0, k, at, :].astype(F32) + gs[k, at, :] + gr[k, at, :])
        for b, block in enumerate(inverse(blocks, ones)):
            minv[pl.ds(8 * b, 8), :] = block

        inv_pair = split(minv[...])
        following = 2 * apart

        @pl.when(k + 1 < levels)
        def _():
            y = split(product(inv_pair, (uh[k], ul[k])))
            gs[k + 1] = cc[k] - product((vh[k], vl[k]), y)

            @pl.when(core == 1)
            def _():
                gram_copy(k + 1, 0, partner_of(following, 1)).start()
                gram_copy(k + 1, 1, partner_of(following, 0)).start()

            uh[k] = y[0]
            ul[k] = y[1]

        proj_copy(k, sibling).wait_recv()
        own = jnp.where(k == 0, ph[core], ps[k])
        alpha = split(product(inv_pair, split(own + pr[k])))

        @pl.when(k + 1 < levels)
        def _():
            ps[k + 1] = product((vh[k], vl[k]), alpha)
            proj_copy(k + 1, partner_of(following, core)).start()

        mixing = split(mix[...])
        acc[...] += product(mixing, alpha)

        @pl.when(k + 1 < levels)
        def _():
            mix[...] = product(mixing, (uh[k], ul[k]))

        return following

    lax.fori_loop(0, levels, level_step, 1)

    swap = pltpu.make_async_remote_copy(
        src_ref=acc, dst_ref=accr, send_sem=sem_a.at[0], recv_sem=sem_a.at[1],
        device_id=(sibling, group), device_id_type=MESH,
    )
    swap.start()
    q_in = (qin[0], qin[1])
    half = pl.ds(pl.multiple_of(core * 128, 128), 128)
    out_ref[:, half] = zh[core] - product(q_in, split(acc[...]))
    swap.wait_recv()
    other = pl.ds(pl.multiple_of((1 - core) * 128, 128), 128)
    out_ref[:, other] = zh[1 - core] - product(q_in, split(accr[...]))

    swap.wait_send()
    gram_copy(0, 0, sibling).wait_send()
    proj_copy(0, sibling).wait_send()
    for level in range(1, levels):
        proj_copy(level, partner_of(1 << level, core)).wait_send()

        @pl.when(core == 1)
        def _():
            gram_copy(level, 0, partner_of(1 << level, 1)).wait_send()
            gram_copy(level, 1, partner_of(1 << level, 0)).wait_send()


def body(rhs_block, leaf_order, leaf_inverse, leaf_basis, transfer, precision):
    points, columns = rhs_block.shape
    rank = leaf_basis.shape[1]
    levels = precision.shape[1]
    half = columns // 2
    vmem = pl.BlockSpec(memory_space=pltpu.VMEM)
    dma = pltpu.SemaphoreType.DMA
    return pl.pallas_call(
        functools.partial(kernel, levels),
        out_shape=jax.ShapeDtypeStruct((points, columns), F32),
        in_specs=[vmem] * 6,
        out_specs=vmem,
        scratch_shapes=[
            pltpu.VMEM((levels, rank, rank), F32),
            pltpu.VMEM((levels, rank, rank), F32),
            pltpu.VMEM((2, rank, half), F32),
            pltpu.VMEM((levels, rank, half), F32),
            pltpu.VMEM((levels, rank, half), F32),
            pltpu.VMEM((levels, rank, rank), BF16),
            pltpu.VMEM((levels, rank, rank), BF16),
            pltpu.VMEM((levels, rank, rank), BF16),
            pltpu.VMEM((levels, rank, rank), BF16),
            pltpu.VMEM((levels, rank, rank), F32),
            pltpu.VMEM((rank, rank), F32),
            pltpu.VMEM((rank, half), F32),
            pltpu.VMEM((rank, rank), F32),
            pltpu.VMEM((rank, half), F32),
            pltpu.VMEM((2, points, half), F32),
            pltpu.VMEM((2, points, rank), BF16),
            pltpu.VMEM((points, points), BF16),
            dma((levels, 2)),
            dma((levels,)),
            dma((levels,)),
            dma((levels,)),
            dma((2,)),
        ],
        compiler_params=pltpu.CompilerParams(collective_id=0, has_side_effects=True, vmem_limit_bytes=48 * 2**20),
        name="tree_solve",
    )(rhs_block, leaf_order, leaf_inverse, leaf_basis, transfer, precision)


def solution(mesh):
    placed = (
        P("leaf", "rhs"),
        P("leaf", None),
        P("leaf", None),
        P("leaf", None),
        P("leaf", None, None, None),
        P("leaf", None, None, None),
    )
    return jax.shard_map(
        body, mesh=mesh, in_specs=placed, out_specs=P("leaf", "rhs"), check_vma=False
    )
```

time: 348 us -> 84.8 us (0.24)
  the two profiles are of different devices: /device:TPU:4 before, /device:TPU:29 now
where the time goes in v1:
time: 84.8 us; the launch traced here: 84.5 us
  Pallas kernels  77.9 us (92%)
  local copies, waits for them, and re-layouts  6.56 us (8%)
    pallas_call x1, Pallas kernels, body(): pl.pallas_call(functools.partial(kernel, levels), out_shape=jax.ShapeDtyp...  77.9 us
    unnamed x13, local copies, waits for them, and re-layouts  6.56 us

profile of v1, /device:TPU:29, one launch (start us, length us, event | category | flops | bytes accessed | tf_op | source)
XLA Modules:
  0.0 84.5 jit_solution(9355851892809769181)
XLA Ops:
  0.0 0.0 copy-start
  0.0 1.2 %copy-done = f32[512,512]{1,0:T(8,128)S(1)} copy-done((f32[512,512]{1,0:T(8,128)S(1)}, f32[512,512]{1,0:T(8,128)}, u32[]{:S(2)}) %copy-start) | copy-done | bytes 1048600
  1.2 0.0 copy-start.1
  1.2 1.0 %copy-done.1 = f32[512,256]{1,0:T(8,128)S(1)} copy-done((f32[512,256]{1,0:T(8,128)S(1)}, f32[512,256]{1,0:T(8,128)}, u32[]{:S(2)}) %copy-start.1) | copy-done | bytes 524312
  2.3 0.0 copy-start.2
  2.3 0.9 %copy-done.2 = f32[512,128]{1,0:T(8,128)S(1)} copy-done((f32[512,128]{1,0:T(8,128)S(1)}, f32[512,128]{1,0:T(8,128)}, u32[]{:S(2)}) %copy-start.2) | copy-done | bytes 262168
  3.2 0.0 copy-start.3
  3.2 0.9 %copy-done.3 = bf16[1,7,128,128]{3,2,1,0:T(8,128)(2,1)S(1)} copy-done((bf16[1,7,128,128]{3,2,1,0:T(8,128)(2,1)S(1)}, bf16[1,7,128,128]{3,2,1,0:T(8,128)(2,1)}, u32[]{:S(2)}) %copy-start.3) | copy-done | bytes 229400
  4.2 0.0 copy-start.4
  4.2 0.9 %copy-done.4 = bf16[1,6,128,128]{3,2,1,0:T(8,128)(2,1)S(1)} copy-done((bf16[1,6,128,128]{3,2,1,0:T(8,128)(2,1)S(1)}, bf16[1,6,128,128]{3,2,1,0:T(8,128)(2,1)}, u32[]{:S(2)}) %copy-start.4) | copy-done | bytes 196632
  5.1 0.0 copy-start.5
  5.1 0.7 copy-done.5
  5.8 77.9 %tree_solve.1 = f32[512,256]{1,0:T(8,128)S(1)} custom-call(f32[512,256]{1,0:T(8,128)S(1)} %copy-done.1, s32[1,512]{1,0:T(1,128)S(1)} %copy-done.5, f32[512,512]{1,0:T(8,128)S(1)} %copy-done, f32[512,128]{1,0:T(8,128)S(1)} %copy-done.2, bf16[1,6,128,128]{3,2,1,0:T(8,128)(2,1)S(1)} %copy-done.4, bf16[1,7,128,128]{3,2,1,0:T(8,128)(2,1)S(1)} %copy-done.3), custom_call_target="tpu_custom_call" | custom-call | tf_op jit(solution)/shard_map/tree_solve/pallas_call | solution.py:242
  83.7 0.8 copy.8
Async XLA Ops:
  0.0 1.2 %copy-start = (f32[512,512]{1,0:T(8,128)S(1)}, f32[512,512]{1,0:T(8,128)}, u32[]{:S(2)}) copy-start(f32[512,512]{1,0:T(8,128)} %inv_ref.1) | copy-start | bytes 3145732
  1.2 1.0 %copy-start.1 = (f32[512,256]{1,0:T(8,128)S(1)}, f32[512,256]{1,0:T(8,128)}, u32[]{:S(2)}) copy-start(f32[512,256]{1,0:T(8,128)} %rhs_ref.1) | copy-start | bytes 1572868
  2.3 0.9 %copy-start.2 = (f32[512,128]{1,0:T(8,128)S(1)}, f32[512,128]{1,0:T(8,128)}, u32[]{:S(2)}) copy-start(f32[512,128]{1,0:T(8,128)} %basis_ref.1) | copy-start | bytes 786436
  3.2 0.9 %copy-start.3 = (bf16[1,7,128,128]{3,2,1,0:T(8,128)(2,1)S(1)}, bf16[1,7,128,128]{3,2,1,0:T(8,128)(2,1)}, u32[]{:S(2)}) copy-start(bf16[1,7,128,128]{3,2,1,0:T(8,128)(2,1)} %precision_ref.1) | copy-start | bytes 688132
  4.2 0.9 %copy-start.4 = (bf16[1,6,128,128]{3,2,1,0:T(8,128)(2,1)S(1)}, bf16[1,6,128,128]{3,2,1,0:T(8,128)(2,1)}, u32[]{:S(2)}) copy-start(bf16[1,6,128,128]{3,2,1,0:T(8,128)(2,1)} %transfer_ref.1) | copy-start | bytes 589828
  5.1 0.7 copy-start.5

commit v2 on v1

v2 whole, which is shorter than its diff:
```python
import functools

import jax
import jax.numpy as jnp
from jax import lax
from jax.experimental import pallas as pl
from jax.experimental.pallas import tpu as pltpu
from jax.sharding import PartitionSpec as P

MESH = pl.DeviceIdType.MESH
F32 = jnp.float32
BF16 = jnp.bfloat16
FLIP = ((0,), (0,))


def split(value):
    high = value.astype(BF16)
    return high, (value - high.astype(F32)).astype(BF16)


def dot(left, right, dims=((1,), (0,))):
    return lax.dot_general(left, right, (dims, ((), ())), preferred_element_type=F32)


def product(left, right, dims=((1,), (0,))):
    left_cat = jnp.concatenate([left[0], left[0], left[1]], axis=dims[0][0])
    right_cat = jnp.concatenate([right[0], right[1], right[0]], axis=dims[1][0])
    return dot(left_cat, right_cat, dims)


def row(value, at):
    return jnp.broadcast_to(value[at : at + 1, :], value.shape)


def total_of(terms):
    while len(terms) > 1:
        terms = [a + b for a, b in zip(terms[::2], terms[1::2])] + ([terms[-1]] if len(terms) % 2 else [])
    return terms[0]


def factors(blocks, ones):
    blocks = list(blocks)
    count = len(blocks)
    width = blocks[0].shape[1]
    sub = lax.broadcasted_iota(jnp.int32, (8, width), 0)
    lane = lax.broadcasted_iota(jnp.int32, (8, width), 1)
    even = sub % 2 == 0
    first, second = [None] * count, [None] * count
    for panel in range(0, count, 2):
        low = 8 * panel
        raw = [
            [jnp.broadcast_to(blocks[b][:, low + j : low + j + 1], (8, width)) for b in range(panel, count)]
            for j in range(16)
        ]
        inside = (lane >= low) & (lane < low + 16)
        unit = [jnp.where(inside, jnp.where(lane - low - 8 * w == sub, 1.0, 0.0), blocks[panel + w]) for w in range(2)]
        z = list(unit)
        cb = [[raw[j][w] * ones for w in range(2)] for j in range(16)]
        straight, cross = [ones, ones], [ones, ones]
        for i in range(0, 16, 2):
            v, s = i // 8, i % 8
            a, b, c = row(cb[i][v], s), row(cb[i + 1][v], s), row(cb[i + 1][v], s + 1)
            r = 1.0 / (a * c - b * b)
            ar, br, cr = a * r, b * r, c * r
            pair = (sub == s) | (sub == s + 1)
            straight[v] = jnp.where(sub == s, cr, jnp.where(sub == s + 1, ar, straight[v]))
            cross[v] = jnp.where(pair, br, cross[v])
            m = []
            for w in range(2):
                m1 = (cb[i][w] * c - cb[i + 1][w] * b) * r
                m2 = (cb[i + 1][w] * a - cb[i][w] * b) * r
                if w == v:
                    m1, m2 = jnp.where(pair, 0.0, m1), jnp.where(pair, 0.0, m2)
                m.append((m1, m2))
            for k in range(i + 2, 16):
                x, y = row(cb[k][v], s), row(cb[k][v], s + 1)
                cb[k] = [cb[k][w] - (m[w][0] * x + m[w][1] * y) for w in range(2)]
            x, y = row(z[v], s), row(z[v], s + 1)
            z = [z[w] - (m[w][0] * x + m[w][1] * y) for w in range(2)]
        done = []
        for w in range(2):
            swapped = jnp.where(even, pltpu.roll(z[w], 7, 0), pltpu.roll(z[w], 1, 0))
            done.append(straight[w] * z[w] - cross[w] * swapped)
        keep = lane < low + 16
        for w in range(2):
            first[panel + w] = jnp.where(keep, unit[w], 0.0)
            second[panel + w] = jnp.where(keep, done[w], 0.0)
        if panel + 2 < count:
            zr = [row(done[j // 8], j % 8) for j in range(16)]
            for b in range(panel + 2, count):
                terms = [raw[j][b - panel] * zr[j] for j in range(16)]
                blocks[b] = jnp.where(inside, 0.0, blocks[b]) - total_of(terms)
    return first, second


def kernel(
    levels, rhs_hbm, order_hbm, inv_hbm, basis_hbm, transfer_hbm, precision_hbm, out_ref,
    rhs_ref, order_ref, inv_ref, basis_ref, transfer_ref, precision_ref,
    gs, gr, ph, ps, pr, pso, po, uh, ul, vh, vl, cc, wv, yh, acc, mix, accr, zh, qin, onehot,
    sem_in, ssem_g, rsem_g, ssem_p, rsem_p, ssem_x, rsem_x,
):
    me = lax.axis_index("leaf")
    group = lax.axis_index("rhs")
    core = me % 2
    sibling = me + 1 - 2 * core
    last = levels - 1
    rank = acc.shape[0]

    def partner_of(apart, target):
        chip_partner = me + apart * (1 - 2 * ((me // apart) % 2))
        return (chip_partner // 2) * 2 + target

    def remote(src, dst, send_sem, recv_sem, target):
        return pltpu.make_async_remote_copy(
            src_ref=src, dst_ref=dst, send_sem=send_sem, recv_sem=recv_sem,
            device_id=(target, group), device_id_type=MESH,
        )

    def gram_copy(level, slot, target):
        return remote(gs.at[level], gr.at[level], ssem_g.at[level, slot], rsem_g.at[level], target)

    def proj_copy(level, target):
        return remote(ps.at[level], pr.at[level], ssem_p.at[level], rsem_p.at[level], target)

    def top_copy(n):
        src = acc if n == 2 else ps.at[last]
        target = sibling if n else partner_of(1 << last, 1 - core)
        return remote(src, (po, pso, accr)[n], ssem_x.at[n], rsem_x.at[n], target)

    loads = [
        pltpu.make_async_copy(src, dst, sem_in.at[n])
        for n, (src, dst) in enumerate((
            (basis_hbm, basis_ref), (inv_hbm, inv_ref), (order_hbm, order_ref), (rhs_hbm, rhs_ref),
            (precision_hbm, precision_ref), (transfer_hbm, transfer_ref),
        ))
    ]
    for load in loads:
        load.start()

    barrier = pltpu.get_barrier_semaphore()

    def tell(target):
        pl.semaphore_signal(barrier, inc=1, device_id=(target, group), device_id_type=MESH)

    tell(sibling)
    for level in range(1, levels):
        tell(partner_of(1 << level, 1))

        @pl.when(core == 0)
        def _():
            tell(partner_of(1 << level, 0))

    @pl.when(core == 1)
    def _():
        tell(partner_of(1 << last, 0))

    loads[0].wait()
    loads[1].wait()
    basis = split(basis_ref[...])
    q_pair = split(product(split(inv_ref[...]), basis))
    gs[0] = product(basis, q_pair, FLIP)

    @pl.when(core == 0)
    def _():
        pl.semaphore_wait(barrier, levels + 1)

    @pl.when(core == 1)
    def _():
        pl.semaphore_wait(barrier, 2 * levels - 1)

    gram_copy(0, 0, sibling).start()

    points = rhs_ref.shape[0]
    loads[2].wait()
    loads[3].wait()
    spread = lax.broadcasted_iota(jnp.int32, (points, points), 0) == order_ref[...]
    onehot[...] = jnp.where(spread, 1.0, 0.0).astype(BF16)
    q_in = (dot(onehot[...], q_pair[0]).astype(BF16), dot(onehot[...], q_pair[1]).astype(BF16))
    qin[0] = q_in[0]
    qin[1] = q_in[1]
    proj = product(q_in, split(rhs_ref[...]), FLIP)
    ph[0] = proj[:, :128]
    ph[1] = proj[:, 128:]
    ps[0] = ph[1 - core]
    proj_copy(0, sibling).start()

    def tables(k, carry):
        mixer = transfer_ref[0, k]
        lam = precision_ref[0, k]
        u = split(dot(lam, mixer))
        v = split(dot(mixer, lam, FLIP))
        uh[k], ul[k] = u
        vh[k], vl[k] = v
        cc[k] = dot(v[0], mixer) + dot(v[1], mixer)
        return carry

    loads[4].wait()
    loads[5].wait()
    lax.fori_loop(0, last, tables, 0)
    ones = jnp.where(basis_ref[:8, :] == basis_ref[:8, :], 1.0, 0.0)
    acc[...] = jnp.zeros_like(acc)
    eye = lax.broadcasted_iota(jnp.int32, (rank, rank), 0) == lax.broadcasted_iota(jnp.int32, (rank, rank), 1)
    mix[...] = jnp.where(eye, 1.0, 0.0)

    def level_step(k, apart):
        following = 2 * apart

        @pl.when(k == last)
        def _():
            q_in = (qin[0], qin[1])
            zh[core] -= product(q_in, split(acc[...]))
            top_copy(2).wait_recv()
            zh[1 - core] -= product(q_in, split(accr[...]))
            q_top = split(product(q_in, split(mix[...])))
            qin[0] = q_top[0]
            qin[1] = q_top[1]

        gram_copy(k, 0, sibling).wait_recv()
        matrix = precision_ref[0, k].astype(F32) + gs[k] + gr[k]
        blocks = [matrix[8 * b : 8 * b + 8, :] for b in range(rank // 8)]
        first, second = factors(blocks, ones)
        w_pair = split(jnp.concatenate(first, axis=0))
        v_pair = split(jnp.concatenate(second, axis=0))
        wv[0], wv[1] = w_pair
        wv[2], wv[3] = v_pair

        @pl.when(k < last)
        def _():
            u_pair = (uh[k], ul[k])
            w_u = split(product((wv[0], wv[1]), u_pair))
            v_u = split(product((wv[2], wv[3]), u_pair))
            gs[k + 1] = cc[k] - product(w_u, v_u, FLIP)

            @pl.when(core == 1)
            def _():
                gram_copy(k + 1, 0, partner_of(following, 1)).start()
                gram_copy(k + 1, 1, partner_of(following, 0)).start()

            yh[0], yh[1] = v_u
            proj_copy(k, sibling).wait_recv()
            own = jnp.where(k == 0, ph[core], ps[k])
            v_s = split(product((wv[2], wv[3]), split(own + pr[k])))
            both = tuple(jnp.concatenate([yh[n], v_s[n]], axis=1) for n in range(2))
            y_alpha = product((wv[0], wv[1]), both, FLIP)
            alpha = split(y_alpha[:, rank:])
            ps[k + 1] = product((vh[k], vl[k]), alpha)
            proj_copy(k + 1, partner_of(following, core)).start()
            turned = split(mix[...])
            acc[...] += product(turned, alpha)

            @pl.when(k + 1 == last)
            def _():
                for n in range(3):
                    top_copy(n).start()

            mix[...] = product(turned, split(y_alpha[:, :rank]))

            @pl.when(k == 2)
            def _():
                rhs = split(rhs_ref[...])
                ordered = tuple(dot(onehot[...], part, FLIP).astype(BF16) for part in rhs)
                z = split(product(split(inv_ref[...]), ordered))
                z_in = dot(onehot[...], z[0]) + dot(onehot[...], z[1])
                zh[0] = z_in[:, :128]
                zh[1] = z_in[:, 128:]

        return following

    lax.fori_loop(0, levels, level_step, 1)

    proj_copy(last, sibling).wait_recv()
    top_copy(0).wait_recv()
    top_copy(1).wait_recv()
    s = split(jnp.concatenate([ps[last] + pr[last], pso[...] + po[...]], axis=1))
    alpha = product((wv[0], wv[1]), split(product((wv[2], wv[3]), s)), FLIP)
    q_top = (qin[0], qin[1])
    for n, part in enumerate((core, 1 - core)):
        at = pl.ds(pl.multiple_of(part * 128, 128), 128)
        out_ref[:, at] = zh[part] - product(q_top, split(alpha[:, 128 * n : 128 * n + 128]))

    gram_copy(0, 0, sibling).wait_send()
    proj_copy(0, sibling).wait_send()
    for level in range(1, levels):
        proj_copy(level, partner_of(1 << level, core)).wait_send()

        @pl.when(core == 1)
        def _():
            gram_copy(level, 0, partner_of(1 << level, 1)).wait_send()
            gram_copy(level, 1, partner_of(1 << level, 0)).wait_send()

    for n in range(3):
        top_copy(n).wait_send()


def body(rhs_block, leaf_order, leaf_inverse, leaf_basis, transfer, precision):
    points, columns = rhs_block.shape
    rank = leaf_basis.shape[1]
    levels = precision.shape[1]
    half = columns // 2
    args = (rhs_block, leaf_order, leaf_inverse, leaf_basis, transfer, precision)
    dma = pltpu.SemaphoreType.DMA
    square = (rank, rank)
    return pl.pallas_call(
        functools.partial(kernel, levels),
        out_shape=jax.ShapeDtypeStruct((points, columns), F32),
        in_specs=[pl.BlockSpec(memory_space=pltpu.HBM)] * 6,
        out_specs=pl.BlockSpec(memory_space=pltpu.VMEM),
        scratch_shapes=[
            *(pltpu.VMEM(arg.shape, arg.dtype) for arg in args),
            pltpu.VMEM((levels, *square), F32),
            pltpu.VMEM((levels, *square), F32),
            pltpu.VMEM((2, rank, half), F32),
            pltpu.VMEM((levels, rank, half), F32),
            pltpu.VMEM((levels, rank, half), F32),
            pltpu.VMEM((rank, half), F32),
            pltpu.VMEM((rank, half), F32),
            pltpu.VMEM((levels, *square), BF16),
            pltpu.VMEM((levels, *square), BF16),
            pltpu.VMEM((levels, *square), BF16),
            pltpu.VMEM((levels, *square), BF16),
            pltpu.VMEM((levels, *square), F32),
            pltpu.VMEM((4, *square), BF16),
            pltpu.VMEM((2, *square), BF16),
            pltpu.VMEM((rank, half), F32),
            pltpu.VMEM(square, F32),
            pltpu.VMEM((rank, half), F32),
            pltpu.VMEM((2, points, half), F32),
            pltpu.VMEM((2, points, rank), BF16),
            pltpu.VMEM((points, points), BF16),
            dma((6,)),
            dma((levels, 2)),
            dma((levels,)),
            dma((levels,)),
            dma((levels,)),
            dma((3,)),
            dma((3,)),
        ],
        compiler_params=pltpu.CompilerParams(collective_id=0, has_side_effects=True, vmem_limit_bytes=60 * 2**20),
        name="tree_solve",
    )(*args)


def solution(mesh):
    placed = (
        P("leaf", "rhs"),
        P("leaf", None),
        P("leaf", None),
        P("leaf", None),
        P("leaf", None, None, None),
        P("leaf", None, None, None),
    )
    return jax.shard_map(
        body, mesh=mesh, in_specs=placed, out_specs=P("leaf", "rhs"), check_vma=False
    )
```

time: 84.8 us -> 71 us (0.84)
  the two profiles are of different devices: /device:TPU:29 before, /device:TPU:66 now
where the time goes in v2:
time: 71 us; the launch traced here: 70.8 us
  Pallas kernels  68.9 us (97%)
  local copies, waits for them, and re-layouts  1.87 us (3%)
    pallas_call x1, Pallas kernels, body(): pl.pallas_call(functools.partial(kernel, levels), out_shape=jax.ShapeDtyp...  68.9 us
    unnamed x1, local copies, waits for them, and re-layouts  1.87 us

profile of v2, /device:TPU:66, one launch (start us, length us, event | category | flops | bytes accessed | tf_op | source)
XLA Modules:
  0.0 70.8 jit_solution(16076334485338515745)
XLA Ops:
  0.0 68.9 %tree_solve.1 = f32[512,256]{1,0:T(8,128)} custom-call(f32[512,256]{1,0:T(8,128)} %rhs_hbm.1, s32[1,512]{1,0:T(1,128)} %order_hbm.1, f32[512,512]{1,0:T(8,128)} %inv_hbm.1, f32[512,128]{1,0:T(8,128)} %basis_hbm.1, bf16[1,6,128,128]{3,2,1,0:T(8,128)(2,1)} %transfer_hbm.1, bf16[1,7,128,128]{3,2,1,0:T(8,128)(2,1)} %precision_hbm.1), custom_call_target="tpu_custom_call" | custom-call | tf_op jit(solution)/shard_map/tree_solve/pallas_call | solution.py:303
  68.9 1.9 %copy.8 = f32[512,256]{1,0:T(8,128)} copy(f32[512,256]{1,0:T(8,128)} %tree_solve.1) | data formatting | bytes 1048576

commit v3 on v2

--- a/solution.py
+++ b/solution.py
@@ -38,18 +38,19 @@
     return terms[0]
 
 
-def factors(blocks, ones):
-    blocks = list(blocks)
-    count = len(blocks)
-    width = blocks[0].shape[1]
+def factors(matrix, ones):
+    count = matrix.shape[0] // 8
+    width = matrix.shape[1]
+    blocks = [matrix[8 * b : 8 * b + 8, :] for b in range(count)]
     sub = lax.broadcasted_iota(jnp.int32, (8, width), 0)
     lane = lax.broadcasted_iota(jnp.int32, (8, width), 1)
     even = sub % 2 == 0
     first, second = [None] * count, [None] * count
     for panel in range(0, count, 2):
         low = 8 * panel
+        near = min(panel + 4, count)
         raw = [
-            [jnp.broadcast_to(blocks[b][:, low + j : low + j + 1], (8, width)) for b in range(panel, count)]
+            [jnp.broadcast_to(blocks[b][:, low + j : low + j + 1], (8, width)) for b in range(panel, near)]
             for j in range(16)
         ]
         inside = (lane >= low) & (lane < low + 16)
@@ -85,11 +86,17 @@
         for w in range(2):
             first[panel + w] = jnp.where(keep, unit[w], 0.0)
             second[panel + w] = jnp.where(keep, done[w], 0.0)
-        if panel + 2 < count:
-            zr = [row(done[j // 8], j % 8) for j in range(16)]
-            for b in range(panel + 2, count):
-                terms = [raw[j][b - panel] * zr[j] for j in range(16)]
-                blocks[b] = jnp.where(inside, 0.0, blocks[b]) - total_of(terms)
+        zr = [row(done[j // 8], j % 8) for j in range(16)]
+        for b in range(panel + 2, near):
+            terms = [raw[j][b - panel] * zr[j] for j in range(16)]
+            blocks[b] = jnp.where(inside, 0.0, blocks[b]) - total_of(terms)
+        if near < count:
+            far = jnp.concatenate(blocks[near:], axis=0)
+            zero = jnp.zeros((8, width), F32)
+            weights = jnp.concatenate([done[b - panel] if 0 <= b - panel < 2 else zero for b in range(count)], axis=0)
+            change = jnp.dot(far, weights, precision=lax.Precision.HIGHEST, preferred_element_type=F32)
+            for n, b in enumerate(range(near, count)):
+                blocks[b] = jnp.where(inside, 0.0, blocks[b]) - change[8 * n : 8 * n + 8, :]
     return first, second
 
 
@@ -196,7 +203,7 @@
 
     loads[4].wait()
     loads[5].wait()
-    lax.fori_loop(0, last, tables, 0)
+    tables(0, 0)
     ones = jnp.where(basis_ref[:8, :] == basis_ref[:8, :], 1.0, 0.0)
     acc[...] = jnp.zeros_like(acc)
     eye = lax.broadcasted_iota(jnp.int32, (rank, rank), 0) == lax.broadcasted_iota(jnp.int32, (rank, rank), 1)
@@ -217,8 +224,7 @@
 
         gram_copy(k, 0, sibling).wait_recv()
         matrix = precision_ref[0, k].astype(F32) + gs[k] + gr[k]
-        blocks = [matrix[8 * b : 8 * b + 8, :] for b in range(rank // 8)]
-        first, second = factors(blocks, ones)
+        first, second = factors(matrix, ones)
         w_pair = split(jnp.concatenate(first, axis=0))
         v_pair = split(jnp.concatenate(second, axis=0))
         wv[0], wv[1] = w_pair
@@ -254,6 +260,14 @@
                     top_copy(n).start()
 
             mix[...] = product(turned, split(y_alpha[:, :rank]))
+
+            @pl.when(k == 0)
+            def _():
+                lax.fori_loop(1, 3, tables, 0)
+
+            @pl.when(k == 1)
+            def _():
+                lax.fori_loop(3, last, tables, 0)
 
             @pl.when(k == 2)
             def _():

time: 71 us -> 66 us (0.930)
  Pallas kernels: 68.9 us -> 64 us
    pallas_call x1, Pallas kernels: 68.9 us -> 64 us  [body(): pl.pallas_call(functools.partial(kernel, levels), out_shape=jax.ShapeDtyp...]
where the time goes in v3:
time: 66 us; the launch traced here: 65.9 us
  Pallas kernels  64 us (97%)
  local copies, waits for them, and re-layouts  1.87 us (3%)
    pallas_call x1, Pallas kernels, body(): pl.pallas_call(functools.partial(kernel, levels), out_shape=jax.ShapeDtyp...  64 us
    unnamed x1, local copies, waits for them, and re-layouts  1.87 us

profile of v3, /device:TPU:66, one launch (start us, length us, event | category | flops | bytes accessed | tf_op | source)
XLA Modules:
  0.0 65.9 jit_solution(6771002328609681578)
XLA Ops:
  0.0 64.0 %tree_solve.1 = f32[512,256]{1,0:T(8,128)} custom-call(f32[512,256]{1,0:T(8,128)} %rhs_hbm.1, s32[1,512]{1,0:T(1,128)} %order_hbm.1, f32[512,512]{1,0:T(8,128)} %inv_hbm.1, f32[512,128]{1,0:T(8,128)} %basis_hbm.1, bf16[1,6,128,128]{3,2,1,0:T(8,128)(2,1)} %transfer_hbm.1, bf16[1,7,128,128]{3,2,1,0:T(8,128)(2,1)} %precision_hbm.1), custom_call_target="tpu_custom_call" | custom-call | tf_op jit(solution)/shard_map/tree_solve/pallas_call | solution.py:317
  64.0 1.9 %copy.8 = f32[512,256]{1,0:T(8,128)} copy(f32[512,256]{1,0:T(8,128)} %tree_solve.1) | data formatting | bytes 1048576

commit v4 on v3

--- a/solution.py
+++ b/solution.py
@@ -101,10 +101,10 @@
 
 
 def kernel(
-    levels, rhs_hbm, order_hbm, inv_hbm, basis_hbm, transfer_hbm, precision_hbm, out_ref,
+    levels, rhs_hbm, order_hbm, inv_hbm, basis_hbm, transfer_hbm, precision_hbm, z_out, q_out, alpha_ref,
     rhs_ref, order_ref, inv_ref, basis_ref, transfer_ref, precision_ref,
-    gs, gr, ph, ps, pr, pso, po, uh, ul, vh, vl, cc, wv, yh, acc, mix, accr, zh, qin, onehot,
-    sem_in, ssem_g, rsem_g, ssem_p, rsem_p, ssem_x, rsem_x,
+    gs, gr, ph, ps, pr, pso, po, uh, ul, vh, vl, cc, wv, yh, acc, mix, accr, zh, qin, qf, onehot,
+    sem_in, sem_out, ssem_g, rsem_g, ssem_p, rsem_p, ssem_x, rsem_x,
 ):
     me = lax.axis_index("leaf")
     group = lax.axis_index("rhs")
@@ -126,6 +126,9 @@
     def gram_copy(level, slot, target):
         return remote(gs.at[level], gr.at[level], ssem_g.at[level, slot], rsem_g.at[level], target)
 
+    def pass_on(level):
+        return remote(gr.at[level], gr.at[level], ssem_g.at[level, 1], rsem_g.at[level], sibling)
+
     def proj_copy(level, target):
         return remote(ps.at[level], pr.at[level], ssem_p.at[level], rsem_p.at[level], target)
 
@@ -133,6 +136,11 @@
         src = acc if n == 2 else ps.at[last]
         target = sibling if n else partner_of(1 << last, 1 - core)
         return remote(src, (po, pso, accr)[n], ssem_x.at[n], rsem_x.at[n], target)
+
+    def result_copy(n):
+        src = qf if n == 2 else zh.at[n]
+        dst = q_out if n == 2 else z_out.at[:, pl.ds(128 * n, 128)]
+        return pltpu.make_async_copy(src, dst, sem_out.at[n])
 
     loads = [
         pltpu.make_async_copy(src, dst, sem_in.at[n])
@@ -151,15 +159,8 @@
 
     tell(sibling)
     for level in range(1, levels):
-        tell(partner_of(1 << level, 1))
-
-        @pl.when(core == 0)
-        def _():
-            tell(partner_of(1 << level, 0))
-
-    @pl.when(core == 1)
-    def _():
-        tell(partner_of(1 << last, 0))
+        tell(partner_of(1 << level, core))
+    tell(partner_of(1 << last, 1 - core))
 
     loads[0].wait()
     loads[1].wait()
@@ -167,14 +168,7 @@
     q_pair = split(product(split(inv_ref[...]), basis))
     gs[0] = product(basis, q_pair, FLIP)
 
-    @pl.when(core == 0)
-    def _():
-        pl.semaphore_wait(barrier, levels + 1)
-
-    @pl.when(core == 1)
-    def _():
-        pl.semaphore_wait(barrier, 2 * levels - 1)
-
+    pl.semaphore_wait(barrier, levels + 1)
     gram_copy(0, 0, sibling).start()
 
     points = rhs_ref.shape[0]
@@ -218,11 +212,16 @@
             zh[core] -= product(q_in, split(acc[...]))
             top_copy(2).wait_recv()
             zh[1 - core] -= product(q_in, split(accr[...]))
-            q_top = split(product(q_in, split(mix[...])))
-            qin[0] = q_top[0]
-            qin[1] = q_top[1]
+            qf[...] = product(q_in, split(mix[...]))
+            for n in range(3):
+                result_copy(n).start()
 
         gram_copy(k, 0, sibling).wait_recv()
+
+        @pl.when((core == 1) & (k > 0) & (k < last))
+        def _():
+            pass_on(k).start()
+
         matrix = precision_ref[0, k].astype(F32) + gs[k] + gr[k]
         first, second = factors(matrix, ones)
         w_pair = split(jnp.concatenate(first, axis=0))
@@ -240,7 +239,10 @@
             @pl.when(core == 1)
             def _():
                 gram_copy(k + 1, 0, partner_of(following, 1)).start()
-                gram_copy(k + 1, 1, partner_of(following, 0)).start()
+
+                @pl.when(k + 1 == last)
+                def _():
+                    gram_copy(last, 1, partner_of(following, 0)).start()
 
             yh[0], yh[1] = v_u
             proj_copy(k, sibling).wait_recv()
@@ -287,11 +289,12 @@
     top_copy(1).wait_recv()
     s = split(jnp.concatenate([ps[last] + pr[last], pso[...] + po[...]], axis=1))
     alpha = product((wv[0], wv[1]), split(product((wv[2], wv[3]), s)), FLIP)
-    q_top = (qin[0], qin[1])
     for n, part in enumerate((core, 1 - core)):
         at = pl.ds(pl.multiple_of(part * 128, 128), 128)
-        out_ref[:, at] = zh[part] - product(q_top, split(alpha[:, 128 * n : 128 * n + 128]))
-
+        alpha_ref[:, at] = alpha[:, 128 * n : 128 * n + 128]
+
+    for n in range(3):
+        result_copy(n).wait()
     gram_copy(0, 0, sibling).wait_send()
     proj_copy(0, sibling).wait_send()
     for level in range(1, levels):
@@ -300,7 +303,10 @@
         @pl.when(core == 1)
         def _():
             gram_copy(level, 0, partner_of(1 << level, 1)).wait_send()
-            gram_copy(level, 1, partner_of(1 << level, 0)).wait_send()
+            if level == last:
+                gram_copy(level, 1, partner_of(1 << level, 0)).wait_send()
+            else:
+                pass_on(level).wait_send()
 
     for n in range(3):
         top_copy(n).wait_send()
@@ -314,11 +320,19 @@
     args = (rhs_block, leaf_order, leaf_inverse, leaf_basis, transfer, precision)
     dma = pltpu.SemaphoreType.DMA
     square = (rank, rank)
-    return pl.pallas_call(
+    z, q, alpha = pl.pallas_call(
         functools.partial(kernel, levels),
-        out_shape=jax.ShapeDtypeStruct((points, columns), F32),
+        out_shape=[
+            jax.ShapeDtypeStruct((points, columns), F32),
+            jax.ShapeDtypeStruct((points, rank), F32),
+            jax.ShapeDtypeStruct((rank, columns), F32),
+        ],
         in_specs=[pl.BlockSpec(memory_space=pltpu.HBM)] * 6,
-        out_specs=pl.BlockSpec(memory_space=pltpu.VMEM),
+        out_specs=[
+            pl.BlockSpec(memory_space=pl.ANY),
+            pl.BlockSpec(memory_space=pl.ANY),
+            pl.BlockSpec(memory_space=pltpu.VMEM),
+        ],
         scratch_shapes=[
             *(pltpu.VMEM(arg.shape, arg.dtype) for arg in args),
             pltpu.VMEM((levels, *square), F32),
@@ -340,8 +354,10 @@
             pltpu.VMEM((rank, half), F32),
             pltpu.VMEM((2, points, half), F32),
             pltpu.VMEM((2, points, rank), BF16),
+            pltpu.VMEM((points, rank), F32),
             pltpu.VMEM((points, points), BF16),
             dma((6,)),
+            dma((3,)),
             dma((levels, 2)),
             dma((levels,)),
             dma((levels,)),
@@ -352,6 +368,7 @@
         compiler_params=pltpu.CompilerParams(collective_id=0, has_side_effects=True, vmem_limit_bytes=60 * 2**20),
         name="tree_solve",
     )(*args)
+    return z - jnp.dot(q, alpha, precision=lax.Precision.HIGHEST, preferred_element_type=F32)
 
 
 def solution(mesh):

time: 66 us -> 66 us (level)
  the two profiles are of different devices: /device:TPU:66 before, /device:TPU:6 now
where the time goes in v4:
time: 66 us; the launch traced here: 65.8 us
  Pallas kernels  63.2 us (96%)
  matrix products  2.56 us (4%)
    pallas_call x1, Pallas kernels, body(): pl.pallas_call(functools.partial(kernel, levels), out_shape=[jax.ShapeDty...  63.2 us
    dot_general x1, matrix products, body(): jnp.dot(q, alpha, precision=lax.Precision.HIGHEST, preferred_element_type...  2.56 us

profile of v4, /device:TPU:6, one launch (start us, length us, event | category | flops | bytes accessed | tf_op | source)
XLA Modules:
  0.0 65.8 jit_solution(10007493366113297646)
XLA Ops:
  0.0 63.2 %tree_solve.1 = (f32[512,256]{1,0:T(8,128)}, f32[512,128]{1,0:T(8,128)}, f32[128,256]{1,0:T(8,128)}) custom-call(f32[512,256]{1,0:T(8,128)} %rhs_hbm.1, s32[1,512]{1,0:T(1,128)} %order_hbm.1, f32[512,512]{1,0:T(8,128)} %inv_hbm.1, f32[512,128]{1,0:T(8,128)} %basis_hbm.1, bf16[1,6,128,128]{3,2,1,0:T(8,128)(2,1)} %transfer_hbm.1, ...), custom_call_target="tpu_custom_call" | custom-call | tf_op jit(solution)/shard_map/tree_solve/pallas_call | solution.py:323
  63.2 2.6 %convolution_subtract_fusion = f32[512,256]{1,0:T(8,128)} fusion(f32[512,256]{1,0:T(8,128)} %get-tuple-element.8, f32[512,128]{1,0:T(8,128)} %get-tuple-element.9, f32[128,256]{1,0:T(8,128)} %get-tuple-element.10), kind=kOutput, calls=%fused_computation | convolution fusion | flops 201457664 | bytes 1441792 | tf_op jit(solution)/shard_map/dot_general | solution.py:371
